TPU v7x, 256 devices: a whole 4x4x8 slice. The times are simulated.
256 devices in a mesh: tm: 8 (over z_hi, x), chan: 32 (over z_lo, y, core).
Axes of the slice: x: 4, y: 4, z: 8 (z_hi: 2, z_lo: 4; z = z_hi * 4 + z_lo), core: 2. Of those that a mesh axis runs over, the one named last changes fastest.
Arguments:
- voltage_frequency_samples: bfloat16 [2, 256, 30, 2, 8192], P(None, ('tm', 'chan')), may hold values from -6 to 6
- lag_lookup_entry: int32 [8, 8, 30], P('tm'), may hold values from 0 to 63
- lag_lookup_turning: float32 [64, 8192], P(None, 'chan'), may hold values from -3.140625 to 3.140625
- antenna_pair_members: int32 [435, 2], replicated, may hold values from 0 to 29, as said below
- frequency_bin_target: int32 [8192], P('chan'), may hold values from 0 to 63, as said below
Outputs:
- centre_vis: float32 [512, 2, 4, 435], P(('tm', 'chan'))
Inputs may be any that keep to these rules, and one draw needn't show every extreme that they name: `antenna_pair_members`: every unordered pair of two different stations of the 30 appears in exactly one row, in either order. `frequency_bin_target`: each of the 64 output channels receives exactly 128 fine channels.
All inputs are finite; a program needn't handle non-finite values.
Results may differ from a plain program's by a relative error of at most 0.0029.
Values may be sent and summed in bfloat16 or wider, within the bound.
A program may use at most 128 MiB of HBM per device.

v0:
```python
import jax
import jax.numpy as jnp
from jax import lax
from jax.sharding import PartitionSpec as P

F = 8192
Q = 64
G_DEV = 1


def correlate(left_part, right_part):
    return jnp.einsum("gtaf,gtbf->gabf", left_part, right_part, preferred_element_type=jnp.float32)


def on_device(
    voltage_frequency_samples,
    lag_lookup_entry,
    lag_lookup_turning,
    antenna_pair_members,
    frequency_bin_target,
):
    regrouped = lax.all_to_all(
        voltage_frequency_samples, "chan", split_axis=4, concat_axis=1, tiled=True
    )
    fine_local = regrouped.shape[4]
    selector = (frequency_bin_target[:, None] == jnp.arange(Q, dtype=jnp.int32)[None, :]).astype(
        jnp.bfloat16
    )
    spectra_count = regrouped.shape[1]
    stations = regrouped.shape[2]
    polars = regrouped.shape[3]
    antenna_pair_total = antenna_pair_members.shape[0]
    shaped = regrouped.reshape(2, G_DEV, spectra_count // G_DEV, stations * polars, fine_local)
    real_part = shaped[0]
    imag_part = shaped[1]
    vis_real = correlate(real_part, real_part) + correlate(imag_part, imag_part)
    vis_imag = correlate(imag_part, real_part) - correlate(real_part, imag_part)
    left_antenna_number = antenna_pair_members[:, 0]
    right_antenna_number = antenna_pair_members[:, 1]
    full_shape = (G_DEV, stations, polars, stations, polars, fine_local)
    picked_real = vis_real.reshape(full_shape)[:, left_antenna_number, :, right_antenna_number]
    picked_imag = vis_imag.reshape(full_shape)[:, left_antenna_number, :, right_antenna_number]
    base_real = jnp.transpose(picked_real, (1, 2, 3, 0, 4)).reshape(
        G_DEV, polars * polars, antenna_pair_total, fine_local
    )
    base_imag = jnp.transpose(picked_imag, (1, 2, 3, 0, 4)).reshape(
        G_DEV, polars * polars, antenna_pair_total, fine_local
    )
    station_phase = jnp.take(lag_lookup_turning, lag_lookup_entry, axis=0)
    phase_diff = (
        station_phase[:, :, left_antenna_number] - station_phase[:, :, right_antenna_number]
    )
    cosine = jnp.cos(phase_diff)
    sine = jnp.sin(phase_diff)
    centres = lag_lookup_entry.shape[1]
    partial_list = []
    for centre in range(centres):
        cos_now = cosine[:, centre][:, None]
        sin_now = sine[:, centre][:, None]
        rot_real = (base_real * cos_now + base_imag * sin_now).astype(jnp.bfloat16)
        rot_imag = (base_imag * cos_now - base_real * sin_now).astype(jnp.bfloat16)
        rotated = jnp.stack([rot_real, rot_imag])
        partial_list.append(
            jnp.einsum("rgpbf,fq->qrpb", rotated, selector, preferred_element_type=jnp.float32)
        )
    partial_value = jnp.stack(partial_list)
    columns = selector.shape[1]
    tail = (2, polars * polars, antenna_pair_total)
    flat = partial_value.reshape((centres * columns,) + tail)
    channel_summed_products = lax.psum_scatter(
        flat, ("tm", "chan"), scatter_dimension=0, tiled=True
    )
    return channel_summed_products * (Q / F)


def solution(mesh):
    return jax.shard_map(
        on_device,
        mesh=mesh,
        in_specs=(
            P(None, ("tm", "chan"), None, None, None),
            P("tm", None, None),
            P(None, "chan"),
            P(),
            P("chan"),
        ),
        out_specs=P(("tm", "chan"), None, None, None),
        check_vma=False,
    )
```

profile of v0, /device:TPU:97, one launch (start us, length us, event | category | flops | bytes accessed | tf_op | source)
XLA Modules:
  0.0 534.2 jit_solution(12457336647658863745)
XLA Ops:
  6.5 19.7 %copy.43 = bf16[2,1,30,2,8192]{2,3,1,0,4:T(2,128)(2,1)} copy(bf16[2,1,30,2,8192]{4,3,2,1,0:T(2,128)(2,1)} %param.5) | data formatting | bytes 3932160 | tf_op args[0]
  26.2 17.3 %reshape.729 = bf16[32,2,15360]{2,1,0:T(2,128)(2,1)} reshape(bf16[8192,2,1,2,30]{4,3,2,1,0:T(2,128)(2,1)} %bitcast.325) | data formatting | bytes 3932160
  43.5 8.3 %all-to-all-start = ((bf16[32,2,15360]{2,1,0:T(2,128)(2,1)}), bf16[32,2,15360]{2,1,0:T(2,128)(2,1)S(1)}, u32[]{:S(2)}, u32[]{:S(2)}) async-start(bf16[32,2,15360]{2,1,0:T(2,128)(2,1)} %reshape.729), calls=%async_computation | async-start | bytes 3932160 | tf_op jit(solution)/shard_map/all_to_all | solution.py:22
  53.6 2.9 gather_fusion.2
  56.5 2.9 gather_fusion.3
  59.4 13.8 %cosine_bitcast_fusion = (f32[1,8,435,256]{3,1,2,0:T(8,128)S(1)}, f32[1,8,435,256]{3,1,2,0:T(8,128)S(1)}) fusion(f32[435,8,256]{2,1,0:T(8,128)} %gather_fusion.2, f32[435,8,256]{2,1,0:T(8,128)} %gather_fusion.3), kind=kLoop, calls=%fused_computation.8 | loop fusion | flops 890880 | bytes 14254080 | tf_op jit(solution)/shard_map/cos | solution.py:53
  73.3 2.4 fusion.99
  76.5 2.4 fusion.98
  91.1 4.9 all-to-all-done
  95.9 24.0 %reshape.730 = bf16[8192,2,1,2,30]{4,3,2,1,0:T(2,128)(2,1)} reshape(bf16[32,2,15360]{2,1,0:T(2,128)(2,1)S(1)} %all-to-all-done) | data formatting | bytes 3932160
  119.9 12.3 %copy.62 = bf16[2,1,30,2,32,256]{5,4,3,2,1,0:T(8,128)(2,1)S(1)} copy(bf16[2,1,30,2,32,256]{2,3,0,5,4,1:T(2,128)(2,1)} %bitcast.324) | data formatting | bytes 3932160 | tf_op jit(solution)/shard_map/all_to_all | solution.py:22
  132.2 1.2 fusion.100
  133.4 5.3 copy.45
  138.7 4.2 copy.47
  142.9 6.9 %fusion.101 = f32[256,60,60]{2,1,0:T(8,128)} fusion(bf16[32,60,256]{1,0,2:T(8,128)(2,1)} %copy.45), kind=kOutput, calls=%fused_computation.169 | convolution fusion | flops 58982400 | bytes 4669440 | tf_op jit(solution)/shard_map/gtaf,gtbf->gabf/dot_general | solution.py:12
  149.8 1.3 fusion.102
  151.2 4.6 subtract_bitcast_fusion
  155.7 8.6 %copy.57 = f32[1,60,60,256]{3,2,1,0:T(8,128)} copy(f32[1,60,60,256]{1,2,3,0:T(8,128)} %subtract_bitcast_fusion) | data formatting | bytes 7372800 | tf_op jit(solution)/shard_map/sub | solution.py:37
  164.3 5.6 %reshape.712 = f32[30,2,30,2,256]{4,3,2,1,0:T(2,128)} reshape(f32[1,60,60,256]{3,2,1,0:T(8,128)} %copy.57) | data formatting | bytes 7372800 | tf_op jit(solution)/shard_map/reshape | solution.py:42
  169.9 8.1 %gather_fusion.4 = f32[435,2,2,256]{3,2,1,0:T(2,128)} fusion(f32[30,2,30,2,256]{4,3,2,1,0:T(2,128)} %reshape.712, s32[435]{0:T(512)S(1)} %bitcast.322), kind=kCustom, calls=%fused_computation.4 | custom fusion | bytes 3567000 | tf_op jit(solution)/shard_map/gather | solution.py:42
  178.0 3.1 copy.58
  181.1 7.9 %add_bitcast_fusion = f32[1,60,60,256]{1,2,3,0:T(8,128)} fusion(f32[256,60,60]{2,1,0:T(8,128)} %fusion.101, bf16[32,60,256]{1,0,2:T(8,128)(2,1)S(1)} %copy.47), kind=kOutput, calls=%fused_computation.6 | convolution fusion | flops 59904000 | bytes 8355840 | tf_op jit(solution)/shard_map/gtaf,gtbf->gabf/dot_general | solution.py:12
  189.1 8.6 %copy.49 = f32[1,60,60,256]{3,2,1,0:T(8,128)} copy(f32[1,60,60,256]{1,2,3,0:T(8,128)} %add_bitcast_fusion) | data formatting | bytes 7372800 | tf_op jit(solution)/shard_map/add | solution.py:36
  197.7 5.6 %reshape.676 = f32[30,2,30,2,256]{4,3,2,1,0:T(2,128)} reshape(f32[1,60,60,256]{3,2,1,0:T(8,128)} %copy.49) | data formatting | bytes 7372800 | tf_op jit(solution)/shard_map/reshape | solution.py:41
  203.4 7.0 %gather_fusion = f32[435,2,2,256]{3,2,1,0:T(2,128)S(1)} fusion(f32[30,2,30,2,256]{4,3,2,1,0:T(2,128)} %reshape.676, s32[435]{0:T(512)S(1)} %bitcast.323), kind=kCustom, calls=%fused_computation | custom fusion | bytes 3567000 | tf_op jit(solution)/shard_map/gather | solution.py:41
  210.8 1.1 copy-done.3
  212.3 7.7 %fusion.53 = (bf16[1,1,4,435,256]{4,3,2,0,1:T(8,128)(2,1)S(1)}, bf16[1,1,4,435,256]{4,3,2,0,1:T(8,128)(2,1)S(1)}, bf16[1,1,4,435,256]{4,3,2,0,1:T(8,128)(2,1)S(1...) fusion(f32[1,2,2,435,256]{4,3,2,1,0:T(8,128)S(1)} %copy-done.3,, ...), kind=kLoop, calls=%fused_computation.86 | loop fusion | flops 28508160 | bytes 24944640 | tf_op jit(solution)/shard_map/convert_element_type | solution.py:60
  220.0 2.2 fusion.71
  226.7 4.3 copy.59
  231.0 12.0 %copy.60 = f32[512,2,4,435]{3,2,1,0:T(4,128)} copy(f32[512,2,4,435]{3,0,2,1:T(8,128)} %bitcast.326) | data formatting | bytes 14254080 | tf_op jit(solution)/shard_map/reshape | solution.py:69
  243.0 282.7 %all-reduce.3.cloned.1.call-done = f32[512,2,4,435]{3,2,1,0:T(4,128)} async-done(((f32[512,2,4,435]{3,2,1,0:T(4,128)}), f32[512,2,4,435]{3,2,1,0:T(4,128)}) %all-reduce.3.cloned.1.call-update) | async-done | bytes 7127056
  525.7 1.4 dynamic-slice_multiply_fusion
  (65 shorter events, 20.1 us)
Async XLA Ops:
  6.5 45.8 %copy-start = (f32[64,256]{1,0:T(8,128)S(1)}, f32[64,256]{1,0:T(8,128)}, u32[]{:S(2)}) copy-start(f32[64,256]{1,0:T(8,128)} %param.7) | copy-start | bytes 196612
  43.5 8.7 %copy-start.12 = (s32[1,8,30]{2,1,0:T(8,128)S(1)}, s32[1,8,30]{2,1,0:T(8,128)}, u32[]{:S(2)}) copy-start(s32[1,8,30]{2,1,0:T(8,128)} %param.6) | copy-start | bytes 2884
  43.5 52.4 %all-to-all-start = ((bf16[32,2,15360]{2,1,0:T(2,128)(2,1)}), bf16[32,2,15360]{2,1,0:T(2,128)(2,1)S(1)}, u32[]{:S(2)}, u32[]{:S(2)}) async-start(bf16[32,2,15360]{2,1,0:T(2,128)(2,1)} %reshape.729), calls=%async_computation | async-start | bytes 3932160 | tf_op jit(solution)/shard_map/all_to_all | solution.py:22
  51.9 1.6 copy-start.13
  51.9 473.8 %all-reduce.3.cloned.1.call-start = ((), (), s32[]{:S(2)}) async-start(), calls=%async_computation.1 | async-start | bytes 16777216
  142.9 6.9 %copy-start.2 = (bf16[32,60,256]{1,0,2:T(8,128)(2,1)S(1)}, bf16[32,60,256]{1,0,2:T(8,128)(2,1)}, u32[]{:S(2)}) copy-start(bf16[32,60,256]{1,0,2:T(8,128)(2,1)} %copy.45) | copy-start | bytes 2949124
  203.3 7.4 %copy-start.8 = (f32[1,1,435,256]{3,2,1,0:T(8,128)S(1)}, f32[1,1,435,256]{3,2,1,0:T(8,128)}, u32[]{:S(2)}) copy-start(f32[1,1,435,256]{3,2,1,0:T(8,128)} %copy.102) | copy-start | bytes 1336324
  203.3 7.4 %copy-start.9 = (f32[1,1,435,256]{3,2,1,0:T(8,128)S(1)}, f32[1,1,435,256]{3,2,1,0:T(8,128)}, u32[]{:S(2)}) copy-start(f32[1,1,435,256]{3,2,1,0:T(8,128)} %copy.103) | copy-start | bytes 1336324
  203.3 7.4 %copy-start.10 = (f32[1,1,435,256]{3,2,1,0:T(8,128)S(1)}, f32[1,1,435,256]{3,2,1,0:T(8,128)}, u32[]{:S(2)}) copy-start(f32[1,1,435,256]{3,2,1,0:T(8,128)} %copy.104) | copy-start | bytes 1336324
  210.4 1.5 copy-start.3
  210.4 1.5 copy-start.4
  210.4 1.7 copy-start.5
  210.4 1.8 copy-start.6
  210.4 1.9 copy-start.7
  212.3 7.7 %copy-start.14 = (s32[256]{0:T(256)S(1)}, s32[256]{0:T(256)}, u32[]{:S(2)}) copy-start(s32[256]{0:T(256)} %param.9) | copy-start | bytes 3076
  220.0 2.2 copy-start.11
  243.0 284.1 %copy-start.1 = (f32[64,256]{1,0:T(8,128)S(1)}, f32[64,256]{1,0:T(8,128)}, u32[]{:S(2)}) copy-start(f32[64,256]{1,0:T(8,128)} %param.7) | copy-start | bytes 196612
Sparse Core Ops, SparseCore 0:
  243.1 282.5 all-reduce.2
where the time goes:
time: 539 us; the launch traced here: 534 us
  waiting for transfers between devices  288 us (53%)
  local copies, waits for them, and re-layouts  173 us (32%)
  matrix products  27.4 us (5%)
  other arithmetic  23.1 us (4%)
  between operations  14 us (3%)
  starting transfers between devices  8.68 us (2%)
    unnamed x2, waiting for transfers between devices  283 us
    unnamed x49, local copies, waits for them, and re-layouts  75.5 us
    dot_general x4, matrix products, correlate(): jnp.einsum('gtaf,gtbf->gabf', left_part, right_part, preferred_element_ty...  20.8 us
    cos x1, other arithmetic, on_device(): cosine = jnp.cos(phase_diff)  13.8 us
    all_to_all x1, local copies, waits for them, and re-layouts, on_device(): lax.all_to_all(voltage_frequency_samples, 'chan', split_axis=4, concat_ax...  12.3 us
    reshape x1, local copies, waits for them, and re-layouts, on_device(): flat = partial_value.reshape((centres * columns,) + tail)  12 us
  transfers between devices with their start and end apart: 2, of which 2 were waited for; matrix products, arithmetic and copies ran while one was open for 7% of the time, Pallas kernels for 0%

commit v1 on v0

--- a/solution.py
+++ b/solution.py
@@ -19,8 +19,14 @@
     antenna_pair_members,
     frequency_bin_target,
 ):
-    regrouped = lax.all_to_all(
-        voltage_frequency_samples, "chan", split_axis=4, concat_axis=1, tiled=True
+    regrouped = jnp.concatenate(
+        lax.all_to_all(
+            jnp.stack(jnp.split(voltage_frequency_samples, lax.axis_size("chan"), axis=4)),
+            "chan",
+            0,
+            0,
+        ),
+        axis=1,
     )
     fine_local = regrouped.shape[4]
     selector = (frequency_bin_target[:, None] == jnp.arange(Q, dtype=jnp.int32)[None, :]).astype(

time: 539 us -> 514 us (0.954)
  local copies, waits for them, and re-layouts: 173 us -> 149 us
    unnamed x49 -> x79, local copies, waits for them, and re-layouts: 75.5 us -> 60.9 us
    all_to_all x1 -> x0, local copies, waits for them, and re-layouts: 12.3 us -> none  [on_device(): lax.all_to_all(voltage_frequency_samples, 'chan', split_axis=4, concat_ax...]
  transfers between devices with their start and end apart: 2 -> 2, of which waited for: 2 -> 2; matrix products, arithmetic and copies ran while one was open for 7% -> 8% of each run, Pallas kernels for 0% -> 0%
where the time goes in v1:
time: 514 us; the launch traced here: 509 us
  waiting for transfers between devices  288 us (56%)
  local copies, waits for them, and re-layouts  149 us (29%)
  matrix products  27.5 us (5%)
  other arithmetic  23.1 us (4%)
  between operations  14 us (3%)
  starting transfers between devices  8.68 us (2%)
    unnamed x2, waiting for transfers between devices  283 us
    unnamed x79, local copies, waits for them, and re-layouts  60.9 us
    dot_general x4, matrix products, correlate(): jnp.einsum('gtaf,gtbf->gabf', left_part, right_part, preferred_element_ty...  20.8 us
    cos x1, other arithmetic, on_device(): cosine = jnp.cos(phase_diff)  13.8 us
    reshape x1, local copies, waits for them, and re-layouts, on_device(): flat = partial_value.reshape((centres * columns,) + tail)  12 us
  transfers between devices with their start and end apart: 2, of which 2 were waited for; matrix products, arithmetic and copies ran while one was open for 8% of the time, Pallas kernels for 0%

profile of v1, /device:TPU:97, one launch (start us, length us, event | category | flops | bytes accessed | tf_op | source)
XLA Modules:
  0.0 509.4 jit_solution(3702456891122394076)
XLA Ops:
  6.5 1.5 constant_dynamic-update-slice_fusion.31
  27.5 1.5 constant_dynamic-update-slice_fusion.17
  37.9 1.5 constant_dynamic-update-slice_fusion.10
  39.4 1.5 constant_dynamic-update-slice_fusion.9
  43.9 1.5 constant_dynamic-update-slice_fusion.6
  45.4 1.5 constant_dynamic-update-slice_fusion.5
  48.4 1.5 constant_dynamic-update-slice_fusion.3
  54.4 8.3 %all-to-all-start = ((bf16[32,2,1,30,2,256]{5,4,3,1,2,0:T(2,128)(2,1)}), bf16[32,2,1,30,2,256]{5,4,3,1,2,0:T(2,128)(2,1)S(1)}, u32[]{:S(2)}, u32[]{:S(2)}) async-start(bf16[32,2,1,30,2,256]{5,4,3,1,2,0:T(2,128)(2,1)} %constant_dynamic-update-slice_fusion), calls=%async_computation | async-start | bytes 3932160 | tf_op jit(solution)/shard_map/all_to_all | solution.py:23
  64.5 2.9 gather_fusion.2
  67.4 2.9 gather_fusion.3
  70.3 13.8 %cosine_bitcast_fusion = (f32[1,8,435,256]{3,1,2,0:T(8,128)S(1)}, f32[1,8,435,256]{3,1,2,0:T(8,128)S(1)}) fusion(f32[435,8,256]{2,1,0:T(8,128)} %gather_fusion.2, f32[435,8,256]{2,1,0:T(8,128)} %gather_fusion.3), kind=kLoop, calls=%fused_computation.8 | loop fusion | flops 890880 | bytes 14254080 | tf_op jit(solution)/shard_map/cos | solution.py:59
  84.2 2.4 fusion.99
  87.4 2.4 fusion.98
  102.0 4.8 all-to-all-done
  106.8 2.1 fusion.100
  109.1 4.4 copy.108
  113.7 4.2 copy.111
  117.9 6.9 %fusion.101 = f32[256,60,60]{2,1,0:T(8,128)} fusion(bf16[32,60,256]{1,0,2:T(8,128)(2,1)} %copy.108), kind=kOutput, calls=%fused_computation.201 | convolution fusion | flops 58982400 | bytes 4669440 | tf_op jit(solution)/shard_map/gtaf,gtbf->gabf/dot_general | solution.py:12
  126.2 4.6 subtract_bitcast_fusion
  130.8 8.6 %copy.121 = f32[1,60,60,256]{3,2,1,0:T(8,128)} copy(f32[1,60,60,256]{1,2,3,0:T(8,128)} %subtract_bitcast_fusion) | data formatting | bytes 7372800 | tf_op jit(solution)/shard_map/sub | solution.py:43
  139.4 5.6 %reshape.714 = f32[30,2,30,2,256]{4,3,2,1,0:T(2,128)} reshape(f32[1,60,60,256]{3,2,1,0:T(8,128)} %copy.121) | data formatting | bytes 7372800 | tf_op jit(solution)/shard_map/reshape | solution.py:48
  145.0 8.1 %gather_fusion.4 = f32[435,2,2,256]{3,2,1,0:T(2,128)} fusion(f32[30,2,30,2,256]{4,3,2,1,0:T(2,128)} %reshape.714, s32[435]{0:T(512)S(1)} %bitcast.383), kind=kCustom, calls=%fused_computation.4 | custom fusion | bytes 3567000 | tf_op jit(solution)/shard_map/gather | solution.py:48
  153.1 3.1 copy.122
  156.2 8.0 %add_bitcast_fusion = f32[1,60,60,256]{1,2,3,0:T(8,128)} fusion(f32[256,60,60]{2,1,0:T(8,128)} %fusion.101, bf16[32,60,256]{1,0,2:T(8,128)(2,1)S(1)} %copy.111), kind=kOutput, calls=%fused_computation.6 | convolution fusion | flops 59904000 | bytes 8355840 | tf_op jit(solution)/shard_map/gtaf,gtbf->gabf/dot_general | solution.py:12
  164.2 8.6 %copy.113 = f32[1,60,60,256]{3,2,1,0:T(8,128)} copy(f32[1,60,60,256]{1,2,3,0:T(8,128)} %add_bitcast_fusion) | data formatting | bytes 7372800 | tf_op jit(solution)/shard_map/add | solution.py:42
  172.8 5.6 %reshape.678 = f32[30,2,30,2,256]{4,3,2,1,0:T(2,128)} reshape(f32[1,60,60,256]{3,2,1,0:T(8,128)} %copy.113) | data formatting | bytes 7372800 | tf_op jit(solution)/shard_map/reshape | solution.py:47
  178.5 7.0 %gather_fusion = f32[435,2,2,256]{3,2,1,0:T(2,128)S(1)} fusion(f32[30,2,30,2,256]{4,3,2,1,0:T(2,128)} %reshape.678, s32[435]{0:T(512)S(1)} %bitcast.384), kind=kCustom, calls=%fused_computation | custom fusion | bytes 3567000 | tf_op jit(solution)/shard_map/gather | solution.py:47
  187.5 7.7 %fusion.53 = (bf16[1,1,4,435,256]{4,3,2,0,1:T(8,128)(2,1)S(1)}, bf16[1,1,4,435,256]{4,3,2,0,1:T(8,128)(2,1)S(1)}, bf16[1,1,4,435,256]{4,3,2,0,1:T(8,128)(2,1)S(1...) fusion(f32[1,2,2,435,256]{4,3,2,1,0:T(8,128)S(1)} %copy-done.3,, ...), kind=kLoop, calls=%fused_computation.86 | loop fusion | flops 28508160 | bytes 24944640 | tf_op jit(solution)/shard_map/convert_element_type | solution.py:66
  195.2 2.2 fusion.71
  201.8 4.3 copy.123
  206.1 12.0 %copy.124 = f32[512,2,4,435]{3,2,1,0:T(4,128)} copy(f32[512,2,4,435]{3,0,2,1:T(8,128)} %bitcast.385) | data formatting | bytes 14254080 | tf_op jit(solution)/shard_map/reshape | solution.py:75
  218.2 282.7 %all-reduce.3.cloned.1.call-done = f32[512,2,4,435]{3,2,1,0:T(4,128)} async-done(((f32[512,2,4,435]{3,2,1,0:T(4,128)}), f32[512,2,4,435]{3,2,1,0:T(4,128)}) %all-reduce.3.cloned.1.call-update) | async-done | bytes 7127056
  (97 shorter events, 61.5 us)
Async XLA Ops:
  6.5 56.7 %copy-start = (f32[64,256]{1,0:T(8,128)S(1)}, f32[64,256]{1,0:T(8,128)}, u32[]{:S(2)}) copy-start(f32[64,256]{1,0:T(8,128)} %param.7) | copy-start | bytes 196612
  54.4 8.7 %copy-start.13 = (s32[1,8,30]{2,1,0:T(8,128)S(1)}, s32[1,8,30]{2,1,0:T(8,128)}, u32[]{:S(2)}) copy-start(s32[1,8,30]{2,1,0:T(8,128)} %param.6) | copy-start | bytes 2884
  54.4 52.4 %all-to-all-start = ((bf16[32,2,1,30,2,256]{5,4,3,1,2,0:T(2,128)(2,1)}), bf16[32,2,1,30,2,256]{5,4,3,1,2,0:T(2,128)(2,1)S(1)}, u32[]{:S(2)}, u32[]{:S(2)}) async-start(bf16[32,2,1,30,2,256]{5,4,3,1,2,0:T(2,128)(2,1)} %constant_dynamic-update-slice_fusion), calls=%async_computation | async-start | bytes 3932160 | tf_op jit(solution)/shard_map/all_to_all | solution.py:23
  62.7 1.6 copy-start.14
  62.7 438.1 %all-reduce.3.cloned.1.call-start = ((), (), s32[]{:S(2)}) async-start(), calls=%async_computation.1 | async-start | bytes 16777216
  109.1 4.4 copy-start.4
  117.9 7.0 %copy-start.2 = (bf16[32,60,256]{1,0,2:T(8,128)(2,1)S(1)}, bf16[32,60,256]{1,0,2:T(8,128)(2,1)}, u32[]{:S(2)}) copy-start(bf16[32,60,256]{1,0,2:T(8,128)(2,1)} %copy.108) | copy-start | bytes 2949124
  178.5 7.4 %copy-start.9 = (f32[1,1,435,256]{3,2,1,0:T(8,128)S(1)}, f32[1,1,435,256]{3,2,1,0:T(8,128)}, u32[]{:S(2)}) copy-start(f32[1,1,435,256]{3,2,1,0:T(8,128)} %copy.165) | copy-start | bytes 1336324
  178.5 7.4 %copy-start.10 = (f32[1,1,435,256]{3,2,1,0:T(8,128)S(1)}, f32[1,1,435,256]{3,2,1,0:T(8,128)}, u32[]{:S(2)}) copy-start(f32[1,1,435,256]{3,2,1,0:T(8,128)} %copy.166) | copy-start | bytes 1336324
  178.5 7.4 %copy-start.11 = (f32[1,1,435,256]{3,2,1,0:T(8,128)S(1)}, f32[1,1,435,256]{3,2,1,0:T(8,128)}, u32[]{:S(2)}) copy-start(f32[1,1,435,256]{3,2,1,0:T(8,128)} %copy.167) | copy-start | bytes 1336324
  185.5 1.5 copy-start.3
  185.5 1.5 copy-start.5
  185.5 1.7 copy-start.6
  185.5 1.8 copy-start.7
  185.5 1.9 copy-start.8
  187.5 7.7 %copy-start.15 = (s32[256]{0:T(256)S(1)}, s32[256]{0:T(256)}, u32[]{:S(2)}) copy-start(s32[256]{0:T(256)} %param.9) | copy-start | bytes 3076
  195.1 2.2 copy-start.12
  218.2 284.1 %copy-start.1 = (f32[64,256]{1,0:T(8,128)S(1)}, f32[64,256]{1,0:T(8,128)}, u32[]{:S(2)}) copy-start(f32[64,256]{1,0:T(8,128)} %param.7) | copy-start | bytes 196612
Sparse Core Ops, SparseCore 0:
  218.3 282.5 all-reduce.2
